TPU v7x, 128 devices: a whole 4x4x4 slice. The times are simulated.
128 devices in a mesh: seq: 4 (over y), grp: 32 (over x, z, core).
Axes of the slice: x: 4, y: 4, z: 4, core: 2. Of those that a mesh axis runs over, the one named last changes fastest.
Arguments:
- basis: bfloat16 [128, 2, 32, 1024], replicated, may hold values from -0.109375 to 0.109375
- background: float32 [32, 4, 2, 2, 32, 1024], P('grp', 'seq'), may hold values from -1.2 to 1.2
- detuning: float32 [32], replicated, may hold values from 1 to 4
- dispersion: float32 [32], replicated, may hold values from 0.5 to 2
- neighbors: int32 [32, 2], replicated, may hold values from 0 to 31, as said below
- step_counts: int32 [32, 4], P('grp', 'seq'), may hold values from 1 to 2
Outputs:
- prefix: float32 [32, 4, 128, 128], P('grp', 'seq')
- monodromy: float32 [128, 128], replicated
Inputs may be any that keep to these rules, and one draw needn't show every extreme that they name: `neighbors`: entry (r, k) is cycle r + d or cycle r - d counted around the closed array of 32 cycles, with 1 <= d <= 3; a cycle may be listed twice in one row.
All inputs are finite; a program needn't handle non-finite values.
Results may differ from a plain program's by a relative error of at most 0.0008.
The roundings to bfloat16 on the way count: a program that leaves them out, or rounds other values in their place, can miss the bound.
Values sent between devices are 32-bit elements; how exact they have to be, the bound alone decides.
A program may use at most 192 MiB of HBM per device.

v0:
```python
import math
import jax
import jax.numpy as jnp
from jax import lax
from jax.sharding import PartitionSpec as P

step_size = 0.1
coupling_rate = 1.0
generator_scale = 0.25


def shifted_2(value, axis, steps):
    count = lax.axis_size(axis)
    first, last = (max(0, -steps), min(count, count - steps))
    return lax.ppermute(value, axis, [(source, source + steps) for source in range(first, last)])


def broadcast(x, axis, root):
    mine = lax.axis_index(axis) == root
    return lax.psum(jnp.where(mine, x, jnp.zeros_like(x)), axis)


def coupling_table(neighbors, cycle_count):
    targets = jnp.arange(cycle_count, dtype=jnp.int32)
    matches = (neighbors[:, :, None] == targets[None, None, :]).astype(jnp.float32)
    return jnp.sum(matches, axis=1)


def propagate(vectors, seg_background, step_total, detuning, dispersion, coupling):
    field_state = vectors
    detune_col = detuning[:, None]
    disp_col = dispersion[:, None]
    for step_index in range(seg_background.shape[0]):
        real_bg = seg_background[step_index, 0]
        imag_bg = seg_background[step_index, 1]
        intensity = 2.0 * (real_bg * real_bg + imag_bg * imag_bg)
        square_re = real_bg * real_bg - imag_bg * imag_bg
        square_im = 2.0 * real_bg * imag_bg
        real_part = field_state[:, 0]
        imag_part = field_state[:, 1]
        lap_re = (
            jnp.roll(real_part, 1, axis=-1) + jnp.roll(real_part, -1, axis=-1) - 2.0 * real_part
        )
        lap_im = (
            jnp.roll(imag_part, 1, axis=-1) + jnp.roll(imag_part, -1, axis=-1) - 2.0 * imag_part
        )
        coupled = jnp.einsum(
            "rm,bcmn->bcrn", coupling, field_state, precision=lax.Precision.HIGHEST
        )
        real_rate = (
            -real_part
            + detune_col * imag_part
            - disp_col * lap_im
            - intensity * imag_part
            - square_im * real_part
            + square_re * imag_part
            - coupling_rate * coupled[:, 1]
        )
        imag_rate = (
            -imag_part
            - detune_col * real_part
            + disp_col * lap_re
            + intensity * real_part
            + square_re * real_part
            + square_im * imag_part
            + coupling_rate * coupled[:, 0]
        )
        advanced = field_state + step_size * jnp.stack([real_rate, imag_rate], axis=1)
        field_state = jnp.where(step_index < step_total, advanced, field_state)
    return field_state


def compose(latter, former):
    return jnp.dot(latter, former, precision=lax.Precision.HIGHEST)


def batch_compose(former, latter):
    return jnp.einsum("bij,bjk->bik", latter, former, precision=lax.Precision.HIGHEST)


def cayley(projected):
    generator = generator_scale * (projected - projected.T)
    identity = jnp.eye(projected.shape[0], dtype=jnp.float32)
    plus_gen = identity + generator
    squared = jnp.dot(plus_gen, plus_gen, precision=lax.Precision.HIGHEST)
    normal = identity + jnp.dot(generator.T, generator, precision=lax.Precision.HIGHEST)
    factor = jnp.linalg.cholesky(normal)
    return jax.scipy.linalg.cho_solve((factor, True), squared)


def shards(basis, background, detuning, dispersion, neighbors, step_counts):
    vec_count = basis.shape[0]
    cycle_count = basis.shape[2]
    sample_count = basis.shape[3]
    coupling = coupling_table(neighbors, cycle_count)
    seg_background = background[0, 0]
    step_total = step_counts[0, 0]
    block_width = math.gcd(vec_count, 32)
    vec_blocks = basis.reshape(vec_count // block_width, block_width, 2, cycle_count, sample_count)
    flat_basis = basis.reshape(vec_count, 2 * cycle_count * sample_count)

    def one_block(vec_block):
        field_state = propagate(
            vec_block.astype(jnp.float32),
            seg_background,
            step_total,
            detuning,
            dispersion,
            coupling,
        )
        propagated = field_state.astype(jnp.bfloat16).reshape(
            block_width, 2 * cycle_count * sample_count
        )
        return lax.dot_general(
            flat_basis, propagated, (((1,), (1,)), ((), ())), preferred_element_type=jnp.float32
        )

    columns = lax.map(one_block, vec_blocks)
    projected = jnp.transpose(columns, (1, 0, 2)).reshape(vec_count, vec_count)
    transfer = cayley(projected)
    identity = jnp.eye(vec_count, dtype=jnp.float32)
    seq_count = lax.axis_size("seq")
    seq_pos = lax.axis_index("seq")
    before = identity
    through = transfer
    for hop_index in range(1, seq_count):
        arrived = shifted_2(through, "seq", 1)
        is_mine = seq_pos == hop_index
        before = jnp.where(is_mine, arrived, before)
        through = jnp.where(is_mine, compose(transfer, arrived), through)
    group_product = broadcast(through, "seq", seq_count - 1)
    grp_count = lax.axis_size("grp")
    grp_pos = lax.axis_index("grp")
    totals = lax.all_gather(group_product[None], "grp", axis=0, tiled=True)
    running = lax.associative_scan(batch_compose, totals)
    monodromy = running[grp_count - 1]
    shifted = jnp.concatenate([identity[None], running[:-1]], axis=0)
    earlier = lax.dynamic_index_in_dim(shifted, grp_pos, 0, keepdims=False)
    prefix = compose(before, earlier)
    return (prefix[None, None], monodromy)


def solution(mesh):
    in_specs = (P(), P("grp", "seq", None, None, None, None), P(), P(), P(), P("grp", "seq"))
    out_specs = (P("grp", "seq", None, None), P())
    return jax.shard_map(shards, mesh=mesh, in_specs=in_specs, out_specs=out_specs, check_vma=False)
```

profile of v0, /device:TPU:1, one launch (start us, length us, event | category | flops | bytes accessed | tf_op | source)
XLA Modules:
  0.0 724.8 jit_solution(4332173955934749635)
XLA Ops:
  9.8 18.7 %copy.70 = bf16[16,8,64,1024]{3,1,2,0:T(8,128)(2,1)} copy(bf16[16,8,64,1024]{3,2,1,0:T(8,128)(2,1)} %bitcast.225) | data formatting | bytes 33554432
  28.6 521.6 %while.13 = (s32[]{:T(128)}, f32[4,128,32]{1,2,0:T(8,128)S(1)}, pred[]{:T(512)}, pred[]{:T(512)}, bf16[4,32,2,32,1024]{4,3,2,1,0:T(8,128)(2,1)}, /*index=5*/f32[...) while((s32[]{:T(128)}, f32[4,128,32]{1,2,0:T(8,128)S(1)}, ...), condition=%wide.region_2.3_spmd, body=%wide.region_1.2_spmd.sunk | while | flops 2248343552 | bytes 402679104 | solution.py:118
  45.0 11.0 %fusion.128 = f32[32,2,32,1024]{3,2,1,0:T(8,128)} fusion(bf16[4,32,2,32,1024]{4,3,2,1,0:T(8,128)(2,1)} %get-tuple-element.440, s32[]{:T(128)} %get-tuple-element.421, f32[32,32]{1,0:T(8,128)S(1)} %get-tuple-element.446), kind=kOutput, calls=%fused_computation.58.clone.1 | convolution fusion | flops 805306368 | bytes 12587520 | tf_op jit(solution)/shard_map/while/body/eval_jaxpr/rm,bcmn->bcrn/dot_general | solution.py:47
  56.7 13.0 %slice_subtract_fusion.4 = (f32[32,1,32,1024]{3,2,1,0:T(8,128)}, f32[32,1,32,1024]{3,2,1,0:T(8,128)}) fusion(f32[32,2,32,1024]{3,2,1,0:T(8,128)} %fusion.128, f32[32,1,32,1023]{3,2,1,0:T(8,128)} %get-tuple-element.377, f32[32,1,32,1]{3,2,1,0:T(8,128)S(1)} %get-tuple-element.378, f32[32,1,32,1]{3,2,1,0:T(8,128)S(1)} %get-tuple-element.379, ...), kind=kLoop, calls=%fused_computation.16.clone.1 | loop fusion | flops 35651584 | bytes 42336512 | tf_op jit(solution)/shard_map/while/body/eval_jaxpr/sub | solution.py:51
  89.2 10.6 %convolution_bitcast_fusion.5 = f32[32,2,32,1024]{3,2,1,0:T(8,128)} fusion(f32[32,2,32,1024]{3,2,1,0:T(8,128)S(1)} %get-tuple-element.389, f32[32,32]{1,0:T(8,128)S(1)} %get-tuple-element.446), kind=kOutput, calls=%fused_computation.57.clone.1 | convolution fusion | flops 805306368 | bytes 16781312 | tf_op jit(solution)/shard_map/while/body/eval_jaxpr/rm,bcmn->bcrn/dot_general | solution.py:47
  99.8 13.1 %slice_subtract_fusion.5 = (f32[32,1,32,1024]{3,2,1,0:T(8,128)}, f32[32,1,32,1024]{3,2,1,0:T(8,128)}) fusion(f32[32,2,32,1024]{3,2,1,0:T(8,128)} %convolution_bitcast_fusion.5, f32[32,1,32,1023]{3,2,1,0:T(8,128)} %get-tuple-element.391, f32[32,1,32,1]{3,2,1,0:T(8,128)S(1)} %get-tuple-element.392, f32[32,1,32,1]{3,2,1,0:T(8,128)S(1)} %get-tuple-element.393, ...), kind=kLoop, calls=%fused_computation.10.clone.1 | loop fusion | flops 35651584 | bytes 42336512 | tf_op jit(solution)/shard_map/while/body/eval_jaxpr/sub | solution.py:51
  141.1 16.0 %fusion.129 = f32[4,128,32]{1,2,0:T(8,128)S(1)} fusion(f32[4,128,32]{1,2,0:T(8,128)S(1)} %get-tuple-element.422, s32[]{:T(128)} %get-tuple-element.421, bf16[128,65536]{1,0:T(8,128)(2,1)} %get-tuple-element.449, f32[32,65536]{1,0:T(8,128)} %bitcast.222, f32[32,65536]{1,0:T(8,128)} %reshape.510, f32[32,65536]{1,0:T(8,128)} %bitcast.223, ...), kind=kOutput, calls=%fused_computation.62.clone.1 | convolution fusion | flops 547356672 | bytes 41959432 | tf_op jit(solution)/shard_map/while/body/eval_jaxpr/dot_general | solution.py:114
  173.6 11.0 %fusion.128 = f32[32,2,32,1024]{3,2,1,0:T(8,128)} fusion(bf16[4,32,2,32,1024]{4,3,2,1,0:T(8,128)(2,1)} %get-tuple-element.440, s32[]{:T(128)} %get-tuple-element.421, f32[32,32]{1,0:T(8,128)S(1)} %get-tuple-element.446), kind=kOutput, calls=%fused_computation.58.clone.1 | convolution fusion | flops 805306368 | bytes 12587520 | tf_op jit(solution)/shard_map/while/body/eval_jaxpr/rm,bcmn->bcrn/dot_general | solution.py:47
  185.3 13.0 %slice_subtract_fusion.4 = (f32[32,1,32,1024]{3,2,1,0:T(8,128)}, f32[32,1,32,1024]{3,2,1,0:T(8,128)}) fusion(f32[32,2,32,1024]{3,2,1,0:T(8,128)} %fusion.128, f32[32,1,32,1023]{3,2,1,0:T(8,128)} %get-tuple-element.377, f32[32,1,32,1]{3,2,1,0:T(8,128)S(1)} %get-tuple-element.378, f32[32,1,32,1]{3,2,1,0:T(8,128)S(1)} %get-tuple-element.379, ...), kind=kLoop, calls=%fused_computation.16.clone.1 | loop fusion | flops 35651584 | bytes 42336512 | tf_op jit(solution)/shard_map/while/body/eval_jaxpr/sub | solution.py:51
  217.6 10.6 %convolution_bitcast_fusion.5 = f32[32,2,32,1024]{3,2,1,0:T(8,128)} fusion(f32[32,2,32,1024]{3,2,1,0:T(8,128)S(1)} %get-tuple-element.389, f32[32,32]{1,0:T(8,128)S(1)} %get-tuple-element.446), kind=kOutput, calls=%fused_computation.57.clone.1 | convolution fusion | flops 805306368 | bytes 16781312 | tf_op jit(solution)/shard_map/while/body/eval_jaxpr/rm,bcmn->bcrn/dot_general | solution.py:47
  228.2 13.4 %slice_subtract_fusion.5 = (f32[32,1,32,1024]{3,2,1,0:T(8,128)}, f32[32,1,32,1024]{3,2,1,0:T(8,128)}) fusion(f32[32,2,32,1024]{3,2,1,0:T(8,128)} %convolution_bitcast_fusion.5, f32[32,1,32,1023]{3,2,1,0:T(8,128)} %get-tuple-element.391, f32[32,1,32,1]{3,2,1,0:T(8,128)S(1)} %get-tuple-element.392, f32[32,1,32,1]{3,2,1,0:T(8,128)S(1)} %get-tuple-element.393, ...), kind=kLoop, calls=%fused_computation.10.clone.1 | loop fusion | flops 35651584 | bytes 42336512 | tf_op jit(solution)/shard_map/while/body/eval_jaxpr/sub | solution.py:51
  269.8 16.0 %fusion.129 = f32[4,128,32]{1,2,0:T(8,128)S(1)} fusion(f32[4,128,32]{1,2,0:T(8,128)S(1)} %get-tuple-element.422, s32[]{:T(128)} %get-tuple-element.421, bf16[128,65536]{1,0:T(8,128)(2,1)} %get-tuple-element.449, f32[32,65536]{1,0:T(8,128)} %bitcast.222, f32[32,65536]{1,0:T(8,128)} %reshape.510, f32[32,65536]{1,0:T(8,128)} %bitcast.223, ...), kind=kOutput, calls=%fused_computation.62.clone.1 | convolution fusion | flops 547356672 | bytes 41959432 | tf_op jit(solution)/shard_map/while/body/eval_jaxpr/dot_general | solution.py:114
  302.0 11.0 %fusion.128 = f32[32,2,32,1024]{3,2,1,0:T(8,128)} fusion(bf16[4,32,2,32,1024]{4,3,2,1,0:T(8,128)(2,1)} %get-tuple-element.440, s32[]{:T(128)} %get-tuple-element.421, f32[32,32]{1,0:T(8,128)S(1)} %get-tuple-element.446), kind=kOutput, calls=%fused_computation.58.clone.1 | convolution fusion | flops 805306368 | bytes 12587520 | tf_op jit(solution)/shard_map/while/body/eval_jaxpr/rm,bcmn->bcrn/dot_general | solution.py:47
  313.7 13.0 %slice_subtract_fusion.4 = (f32[32,1,32,1024]{3,2,1,0:T(8,128)}, f32[32,1,32,1024]{3,2,1,0:T(8,128)}) fusion(f32[32,2,32,1024]{3,2,1,0:T(8,128)} %fusion.128, f32[32,1,32,1023]{3,2,1,0:T(8,128)} %get-tuple-element.377, f32[32,1,32,1]{3,2,1,0:T(8,128)S(1)} %get-tuple-element.378, f32[32,1,32,1]{3,2,1,0:T(8,128)S(1)} %get-tuple-element.379, ...), kind=kLoop, calls=%fused_computation.16.clone.1 | loop fusion | flops 35651584 | bytes 42336512 | tf_op jit(solution)/shard_map/while/body/eval_jaxpr/sub | solution.py:51
  346.3 10.6 %convolution_bitcast_fusion.5 = f32[32,2,32,1024]{3,2,1,0:T(8,128)} fusion(f32[32,2,32,1024]{3,2,1,0:T(8,128)S(1)} %get-tuple-element.389, f32[32,32]{1,0:T(8,128)S(1)} %get-tuple-element.446), kind=kOutput, calls=%fused_computation.57.clone.1 | convolution fusion | flops 805306368 | bytes 16781312 | tf_op jit(solution)/shard_map/while/body/eval_jaxpr/rm,bcmn->bcrn/dot_general | solution.py:47
  356.9 13.1 %slice_subtract_fusion.5 = (f32[32,1,32,1024]{3,2,1,0:T(8,128)}, f32[32,1,32,1024]{3,2,1,0:T(8,128)}) fusion(f32[32,2,32,1024]{3,2,1,0:T(8,128)} %convolution_bitcast_fusion.5, f32[32,1,32,1023]{3,2,1,0:T(8,128)} %get-tuple-element.391, f32[32,1,32,1]{3,2,1,0:T(8,128)S(1)} %get-tuple-element.392, f32[32,1,32,1]{3,2,1,0:T(8,128)S(1)} %get-tuple-element.393, ...), kind=kLoop, calls=%fused_computation.10.clone.1 | loop fusion | flops 35651584 | bytes 42336512 | tf_op jit(solution)/shard_map/while/body/eval_jaxpr/sub | solution.py:51
  398.2 16.0 %fusion.129 = f32[4,128,32]{1,2,0:T(8,128)S(1)} fusion(f32[4,128,32]{1,2,0:T(8,128)S(1)} %get-tuple-element.422, s32[]{:T(128)} %get-tuple-element.421, bf16[128,65536]{1,0:T(8,128)(2,1)} %get-tuple-element.449, f32[32,65536]{1,0:T(8,128)} %bitcast.222, f32[32,65536]{1,0:T(8,128)} %reshape.510, f32[32,65536]{1,0:T(8,128)} %bitcast.223, ...), kind=kOutput, calls=%fused_computation.62.clone.1 | convolution fusion | flops 547356672 | bytes 41959432 | tf_op jit(solution)/shard_map/while/body/eval_jaxpr/dot_general | solution.py:114
  430.7 11.0 %fusion.128 = f32[32,2,32,1024]{3,2,1,0:T(8,128)} fusion(bf16[4,32,2,32,1024]{4,3,2,1,0:T(8,128)(2,1)} %get-tuple-element.440, s32[]{:T(128)} %get-tuple-element.421, f32[32,32]{1,0:T(8,128)S(1)} %get-tuple-element.446), kind=kOutput, calls=%fused_computation.58.clone.1 | convolution fusion | flops 805306368 | bytes 12587520 | tf_op jit(solution)/shard_map/while/body/eval_jaxpr/rm,bcmn->bcrn/dot_general | solution.py:47
  442.3 13.0 %slice_subtract_fusion.4 = (f32[32,1,32,1024]{3,2,1,0:T(8,128)}, f32[32,1,32,1024]{3,2,1,0:T(8,128)}) fusion(f32[32,2,32,1024]{3,2,1,0:T(8,128)} %fusion.128, f32[32,1,32,1023]{3,2,1,0:T(8,128)} %get-tuple-element.377, f32[32,1,32,1]{3,2,1,0:T(8,128)S(1)} %get-tuple-element.378, f32[32,1,32,1]{3,2,1,0:T(8,128)S(1)} %get-tuple-element.379, ...), kind=kLoop, calls=%fused_computation.16.clone.1 | loop fusion | flops 35651584 | bytes 42336512 | tf_op jit(solution)/shard_map/while/body/eval_jaxpr/sub | solution.py:51
  485.3 13.4 %slice_subtract_fusion.5 = (f32[32,1,32,1024]{3,2,1,0:T(8,128)}, f32[32,1,32,1024]{3,2,1,0:T(8,128)}) fusion(f32[32,2,32,1024]{3,2,1,0:T(8,128)} %convolution_bitcast_fusion.5, f32[32,1,32,1023]{3,2,1,0:T(8,128)} %get-tuple-element.391, f32[32,1,32,1]{3,2,1,0:T(8,128)S(1)} %get-tuple-element.392, f32[32,1,32,1]{3,2,1,0:T(8,128)S(1)} %get-tuple-element.393, ...), kind=kLoop, calls=%fused_computation.10.clone.1 | loop fusion | flops 35651584 | bytes 42336512 | tf_op jit(solution)/shard_map/while/body/eval_jaxpr/sub | solution.py:51
  526.8 16.0 %fusion.129 = f32[4,128,32]{1,2,0:T(8,128)S(1)} fusion(f32[4,128,32]{1,2,0:T(8,128)S(1)} %get-tuple-element.422, s32[]{:T(128)} %get-tuple-element.421, bf16[128,65536]{1,0:T(8,128)(2,1)} %get-tuple-element.449, f32[32,65536]{1,0:T(8,128)} %bitcast.222, f32[32,65536]{1,0:T(8,128)} %reshape.510, f32[32,65536]{1,0:T(8,128)} %bitcast.223, ...), kind=kOutput, calls=%fused_computation.62.clone.1 | convolution fusion | flops 547356672 | bytes 41959432 | tf_op jit(solution)/shard_map/while/body/eval_jaxpr/dot_general | solution.py:114
  551.0 11.7 %cholesky.19 = f32[128,128]{1,0:T(8,128)S(1)} custom-call(f32[128,128]{1,0:T(8,128)S(1)} %fusion.77), custom_call_target="Cholesky" | custom-call | tf_op jit(solution)/shard_map/jit(cholesky)/cholesky | solution.py:87
  591.1 45.2 %all-reduce.12.cloned.1.call-done = f32[1,128,128]{2,1,0:T(8,128)} async-done(((f32[1,128,128]{2,1,0:T(8,128)}), f32[1,128,128]{2,1,0:T(8,128)}) %all-reduce.12.cloned.1.call-update) | async-done | bytes 65552 | tf_op jit(solution)/shard_map/psum | solution.py:20
  636.3 49.3 %all-gather.2.cloned.1.call-done = f32[32,128,128]{2,1,0:T(8,128)} async-done(((f32[1,128,128]{2,1,0:T(8,128)}), f32[32,128,128]{2,1,0:T(8,128)}) %all-gather.2.cloned.1.call-update) | async-done | bytes 2097168 | tf_op jit(solution)/shard_map/all_gather | solution.py:134
  (189 shorter events, 330.3 us)
Async XLA Ops:
  7.2 629.1 %all-reduce.12.cloned.1.call-start = ((), (), s32[]{:S(2)}) async-start(), calls=%async_computation | async-start | bytes 131072 | tf_op jit(solution)/shard_map/psum | solution.py:20
  9.7 18.8 %copy-start.7 = (s32[32,2]{0,1:T(2,128)S(1)}, s32[32,2]{0,1:T(2,128)}, u32[]{:S(2)}) copy-start(s32[32,2]{0,1:T(2,128)} %param.12) | copy-start | bytes 772
  9.8 18.8 %copy-start = (f32[1,1,2,2,32,1024]{5,4,3,2,1,0:T(8,128)S(1)}, f32[1,1,2,2,32,1024]{5,4,3,2,1,0:T(8,128)}, u32[]{:S(2)}) copy-start(f32[1,1,2,2,32,1024]{5,4,3,2,1,0:T(8,128)} %param.9) | copy-start | bytes 1572868
  9.8 18.8 %copy-start.6 = (f32[32]{0:T(128)S(1)}, f32[32]{0:T(128)}, u32[]{:S(2)}) copy-start(f32[32]{0:T(128)} %param.10) | copy-start | bytes 388
  29.0 27.0 %copy-start.3 = (f32[1,32,1024]{2,1,0:T(8,128)}, f32[1,32,1024]{2,1,0:T(8,128)S(1)}, u32[]{:S(2)}) copy-start(f32[1,32,1024]{2,1,0:T(8,128)S(1)} %get-tuple-element.447) | copy-start | bytes 393220 | tf_op jit(solution)/shard_map/while
  45.0 11.0 %copy-start.5 = (f32[1,32,1024]{2,1,0:T(8,128)S(1)}, f32[1,32,1024]{2,1,0:T(8,128)}, u32[]{:S(2)}) copy-start(f32[1,32,1024]{2,1,0:T(8,128)} %get-tuple-element.443) | copy-start | bytes 393220 | tf_op jit(solution)/shard_map/while
  89.2 10.6 %copy-start.2 = (f32[1,32,1024]{2,1,0:T(8,128)S(1)}, f32[1,32,1024]{2,1,0:T(8,128)}, u32[]{:S(2)}) copy-start(f32[1,32,1024]{2,1,0:T(8,128)} %get-tuple-element.448) | copy-start | bytes 393220 | tf_op jit(solution)/shard_map/while
  141.1 16.0 %copy-start.4 = (f32[1,32,1024]{2,1,0:T(8,128)S(1)}, f32[1,32,1024]{2,1,0:T(8,128)}, u32[]{:S(2)}) copy-start(f32[1,32,1024]{2,1,0:T(8,128)} %copy-done.3) | copy-start | bytes 393220 | tf_op jit(solution)/shard_map/while
  157.6 27.0 %copy-start.3 = (f32[1,32,1024]{2,1,0:T(8,128)}, f32[1,32,1024]{2,1,0:T(8,128)S(1)}, u32[]{:S(2)}) copy-start(f32[1,32,1024]{2,1,0:T(8,128)S(1)} %get-tuple-element.447) | copy-start | bytes 393220 | tf_op jit(solution)/shard_map/while
  173.6 11.0 %copy-start.5 = (f32[1,32,1024]{2,1,0:T(8,128)S(1)}, f32[1,32,1024]{2,1,0:T(8,128)}, u32[]{:S(2)}) copy-start(f32[1,32,1024]{2,1,0:T(8,128)} %get-tuple-element.443) | copy-start | bytes 393220 | tf_op jit(solution)/shard_map/while
  217.6 10.6 %copy-start.2 = (f32[1,32,1024]{2,1,0:T(8,128)S(1)}, f32[1,32,1024]{2,1,0:T(8,128)}, u32[]{:S(2)}) copy-start(f32[1,32,1024]{2,1,0:T(8,128)} %get-tuple-element.448) | copy-start | bytes 393220 | tf_op jit(solution)/shard_map/while
  269.8 16.0 %copy-start.4 = (f32[1,32,1024]{2,1,0:T(8,128)S(1)}, f32[1,32,1024]{2,1,0:T(8,128)}, u32[]{:S(2)}) copy-start(f32[1,32,1024]{2,1,0:T(8,128)} %copy-done.3) | copy-start | bytes 393220 | tf_op jit(solution)/shard_map/while
  286.0 27.0 %copy-start.3 = (f32[1,32,1024]{2,1,0:T(8,128)}, f32[1,32,1024]{2,1,0:T(8,128)S(1)}, u32[]{:S(2)}) copy-start(f32[1,32,1024]{2,1,0:T(8,128)S(1)} %get-tuple-element.447) | copy-start | bytes 393220 | tf_op jit(solution)/shard_map/while
  302.0 11.0 %copy-start.5 = (f32[1,32,1024]{2,1,0:T(8,128)S(1)}, f32[1,32,1024]{2,1,0:T(8,128)}, u32[]{:S(2)}) copy-start(f32[1,32,1024]{2,1,0:T(8,128)} %get-tuple-element.443) | copy-start | bytes 393220 | tf_op jit(solution)/shard_map/while
  346.3 10.6 %copy-start.2 = (f32[1,32,1024]{2,1,0:T(8,128)S(1)}, f32[1,32,1024]{2,1,0:T(8,128)}, u32[]{:S(2)}) copy-start(f32[1,32,1024]{2,1,0:T(8,128)} %get-tuple-element.448) | copy-start | bytes 393220 | tf_op jit(solution)/shard_map/while
  398.2 16.0 %copy-start.4 = (f32[1,32,1024]{2,1,0:T(8,128)S(1)}, f32[1,32,1024]{2,1,0:T(8,128)}, u32[]{:S(2)}) copy-start(f32[1,32,1024]{2,1,0:T(8,128)} %copy-done.3) | copy-start | bytes 393220 | tf_op jit(solution)/shard_map/while
  414.6 27.0 %copy-start.3 = (f32[1,32,1024]{2,1,0:T(8,128)}, f32[1,32,1024]{2,1,0:T(8,128)S(1)}, u32[]{:S(2)}) copy-start(f32[1,32,1024]{2,1,0:T(8,128)S(1)} %get-tuple-element.447) | copy-start | bytes 393220 | tf_op jit(solution)/shard_map/while
  430.7 11.0 %copy-start.5 = (f32[1,32,1024]{2,1,0:T(8,128)S(1)}, f32[1,32,1024]{2,1,0:T(8,128)}, u32[]{:S(2)}) copy-start(f32[1,32,1024]{2,1,0:T(8,128)} %get-tuple-element.443) | copy-start | bytes 393220 | tf_op jit(solution)/shard_map/while
  474.7 10.6 %copy-start.2 = (f32[1,32,1024]{2,1,0:T(8,128)S(1)}, f32[1,32,1024]{2,1,0:T(8,128)}, u32[]{:S(2)}) copy-start(f32[1,32,1024]{2,1,0:T(8,128)} %get-tuple-element.448) | copy-start | bytes 393220 | tf_op jit(solution)/shard_map/while
  526.8 16.0 %copy-start.4 = (f32[1,32,1024]{2,1,0:T(8,128)S(1)}, f32[1,32,1024]{2,1,0:T(8,128)}, u32[]{:S(2)}) copy-start(f32[1,32,1024]{2,1,0:T(8,128)} %copy-done.3) | copy-start | bytes 393220 | tf_op jit(solution)/shard_map/while
  574.4 5.4 collective-permute-start
  579.9 5.0 collective-permute-start.1
  585.1 5.0 collective-permute-start.2
  591.0 94.6 %all-gather.2.cloned.1.call-start = ((), (), s32[]{:S(2)}) async-start(), calls=%async_computation.1 | async-start | bytes 2162688 | tf_op jit(solution)/shard_map/all_gather | solution.py:134
  (10 other events, 81.5 us)
Sparse Core Ops, SparseCore 0:
  591.1 45.1 all-reduce.11
  638.8 46.7 all-gather.1
where the time goes:
time: 728 us; the launch traced here: 725 us
  local copies, waits for them, and re-layouts  215 us (30%)
  other arithmetic  214 us (29%)
  matrix products  161 us (22%)
  waiting for transfers between devices  98.4 us (14%)
  between operations  15.4 us (2%)
  starting transfers between devices  11.5 us (2%)
  loops' own time  9.17 us (1%)
    sub x8, other arithmetic, propagate(): -real_part + detune_col * imag_part - disp_col * lap_im  105 us
    dot_general x8, matrix products, propagate(): jnp.einsum('rm,bcmn->bcrn', coupling, field_state, precision=lax.Precisio...  86.4 us
    while x56, local copies, waits for them, and re-layouts  64.8 us
    dot_general x4, matrix products, one_block(): lax.dot_general(flat_basis, propagated, (((1,), (1,)), ((), ())), preferr...  64 us
    mul x8, other arithmetic, propagate(): step_size * jnp.stack([real_rate, imag_rate], axis=1)  50.1 us
    concatenate x16, local copies, waits for them, and re-layouts, propagate(): jnp.roll(real_part, -1, axis=-1)  49.4 us
    all_gather x1, waiting for transfers between devices, shards(): totals = lax.all_gather(group_product[None], 'grp', axis=0, tiled=True)  49.3 us
    psum x1, waiting for transfers between devices, broadcast(): return lax.psum(jnp.where(mine, x, jnp.zeros_like(x)), axis)  45.2 us
  transfers between devices with their start and end apart: 5, of which 5 were waited for; matrix products, arithmetic and copies ran while one was open for 0% of the time, Pallas kernels for 0%

commit v1 on v0

--- a/solution.py
+++ b/solution.py
@@ -17,7 +17,7 @@
 
 def broadcast(x, axis, root):
     mine = lax.axis_index(axis) == root
-    return lax.psum(jnp.where(mine, x, jnp.zeros_like(x)), axis)
+    return jnp.sum(lax.all_gather(jnp.where(mine, x, jnp.zeros_like(x)), axis), axis=0)
 
 
 def coupling_table(neighbors, cycle_count):

time: 728 us -> 693 us (0.952)
  waiting for transfers between devices: 98.4 us -> 56.4 us
  blocking collectives: 0 us -> 11 us
    psum x1 -> x0, waiting for transfers between devices: 45.2 us -> none  [broadcast(): return lax.psum(jnp.where(mine, x, jnp.zeros_like(x)), axis)]
    all_gather x0 -> x1, blocking collectives: none -> 11 us  [broadcast(): lax.all_gather(jnp.where(mine, x, jnp.zeros_like(x)), axis)]
    unnamed x10 -> x8, local copies, waits for them, and re-layouts: 25.1 us -> 25 us
  transfers between devices with their start and end apart: 5 -> 4, of which waited for: 5 -> 4; matrix products, arithmetic and copies ran while one was open for 0% -> 0% of each run, Pallas kernels for 0% -> 0%
where the time goes in v1:
time: 693 us; the launch traced here: 690 us
  other arithmetic  216 us (31%)
  local copies, waits for them, and re-layouts  210 us (30%)
  matrix products  161 us (23%)
  waiting for transfers between devices  56.4 us (8%)
  between operations  15.4 us (2%)
  starting transfers between devices  11.5 us (2%)
  blocking collectives  11 us (2%)
  loops' own time  9.21 us (1%)
    sub x8, other arithmetic, propagate(): -real_part + detune_col * imag_part - disp_col * lap_im  105 us
    dot_general x8, matrix products, propagate(): jnp.einsum('rm,bcmn->bcrn', coupling, field_state, precision=lax.Precisio...  86.5 us
    while x56, local copies, waits for them, and re-layouts  64.7 us
    dot_general x4, matrix products, one_block(): lax.dot_general(flat_basis, propagated, (((1,), (1,)), ((), ())), preferr...  64 us
    all_gather x1, waiting for transfers between devices, shards(): totals = lax.all_gather(group_product[None], 'grp', axis=0, tiled=True)  52.5 us
    mul x8, other arithmetic, propagate(): step_size * jnp.stack([real_rate, imag_rate], axis=1)  50 us
    concatenate x16, local copies, waits for them, and re-layouts, propagate(): jnp.roll(real_part, -1, axis=-1)  49.3 us
    convert_element_type x4, local copies, waits for them, and re-layouts, one_block(): vec_block.astype(jnp.float32)  29.8 us
  transfers between devices with their start and end apart: 4, of which 4 were waited for; matrix products, arithmetic and copies ran while one was open for 0% of the time, Pallas kernels for 0%

profile of v1, /device:TPU:1, one launch (start us, length us, event | category | flops | bytes accessed | tf_op | source)
XLA Modules:
  0.0 690.2 jit_solution(129521264530115814)
XLA Ops:
  9.8 18.7 %copy.58 = bf16[16,8,64,1024]{3,1,2,0:T(8,128)(2,1)} copy(bf16[16,8,64,1024]{3,2,1,0:T(8,128)(2,1)} %bitcast.227) | data formatting | bytes 33554432
  28.6 521.3 %while.13 = (s32[]{:T(128)}, f32[4,128,32]{1,2,0:T(8,128)S(1)}, pred[]{:T(512)}, pred[]{:T(512)}, bf16[4,32,2,32,1024]{4,3,2,1,0:T(8,128)(2,1)}, /*index=5*/f32[...) while((s32[]{:T(128)}, f32[4,128,32]{1,2,0:T(8,128)S(1)}, ...), condition=%wide.region_2.3_spmd, body=%wide.region_1.2_spmd.sunk | while | flops 2248343552 | bytes 402679104 | solution.py:118
  44.9 11.0 %fusion.127 = f32[32,2,32,1024]{3,2,1,0:T(8,128)} fusion(bf16[4,32,2,32,1024]{4,3,2,1,0:T(8,128)(2,1)} %get-tuple-element.440, s32[]{:T(128)} %get-tuple-element.421, f32[32,32]{1,0:T(8,128)S(1)} %get-tuple-element.446), kind=kOutput, calls=%fused_computation.58.clone.1 | convolution fusion | flops 805306368 | bytes 12587520 | tf_op jit(solution)/shard_map/while/body/eval_jaxpr/rm,bcmn->bcrn/dot_general | solution.py:47
  56.6 13.0 %slice_subtract_fusion.4 = (f32[32,1,32,1024]{3,2,1,0:T(8,128)}, f32[32,1,32,1024]{3,2,1,0:T(8,128)}) fusion(f32[32,2,32,1024]{3,2,1,0:T(8,128)} %fusion.127, f32[32,1,32,1023]{3,2,1,0:T(8,128)} %get-tuple-element.377, f32[32,1,32,1]{3,2,1,0:T(8,128)S(1)} %get-tuple-element.378, f32[32,1,32,1]{3,2,1,0:T(8,128)S(1)} %get-tuple-element.379, ...), kind=kLoop, calls=%fused_computation.16.clone.1 | loop fusion | flops 35651584 | bytes 42336512 | tf_op jit(solution)/shard_map/while/body/eval_jaxpr/sub | solution.py:51
  89.1 10.6 %convolution_bitcast_fusion.5 = f32[32,2,32,1024]{3,2,1,0:T(8,128)} fusion(f32[32,2,32,1024]{3,2,1,0:T(8,128)S(1)} %get-tuple-element.389, f32[32,32]{1,0:T(8,128)S(1)} %get-tuple-element.446), kind=kOutput, calls=%fused_computation.57.clone.1 | convolution fusion | flops 805306368 | bytes 16781312 | tf_op jit(solution)/shard_map/while/body/eval_jaxpr/rm,bcmn->bcrn/dot_general | solution.py:47
  99.7 13.1 %slice_subtract_fusion.5 = (f32[32,1,32,1024]{3,2,1,0:T(8,128)}, f32[32,1,32,1024]{3,2,1,0:T(8,128)}) fusion(f32[32,2,32,1024]{3,2,1,0:T(8,128)} %convolution_bitcast_fusion.5, f32[32,1,32,1023]{3,2,1,0:T(8,128)} %get-tuple-element.391, f32[32,1,32,1]{3,2,1,0:T(8,128)S(1)} %get-tuple-element.392, f32[32,1,32,1]{3,2,1,0:T(8,128)S(1)} %get-tuple-element.393, ...), kind=kLoop, calls=%fused_computation.10.clone.1 | loop fusion | flops 35651584 | bytes 42336512 | tf_op jit(solution)/shard_map/while/body/eval_jaxpr/sub | solution.py:51
  141.0 16.0 %fusion.128 = f32[4,128,32]{1,2,0:T(8,128)S(1)} fusion(f32[4,128,32]{1,2,0:T(8,128)S(1)} %get-tuple-element.422, s32[]{:T(128)} %get-tuple-element.421, bf16[128,65536]{1,0:T(8,128)(2,1)} %get-tuple-element.449, f32[32,65536]{1,0:T(8,128)} %bitcast.224, f32[32,65536]{1,0:T(8,128)} %reshape.513, f32[32,65536]{1,0:T(8,128)} %bitcast.225, ...), kind=kOutput, calls=%fused_computation.62.clone.1 | convolution fusion | flops 547356672 | bytes 41959432 | tf_op jit(solution)/shard_map/while/body/eval_jaxpr/dot_general | solution.py:114
  173.5 11.0 %fusion.127 = f32[32,2,32,1024]{3,2,1,0:T(8,128)} fusion(bf16[4,32,2,32,1024]{4,3,2,1,0:T(8,128)(2,1)} %get-tuple-element.440, s32[]{:T(128)} %get-tuple-element.421, f32[32,32]{1,0:T(8,128)S(1)} %get-tuple-element.446), kind=kOutput, calls=%fused_computation.58.clone.1 | convolution fusion | flops 805306368 | bytes 12587520 | tf_op jit(solution)/shard_map/while/body/eval_jaxpr/rm,bcmn->bcrn/dot_general | solution.py:47
  185.2 13.0 %slice_subtract_fusion.4 = (f32[32,1,32,1024]{3,2,1,0:T(8,128)}, f32[32,1,32,1024]{3,2,1,0:T(8,128)}) fusion(f32[32,2,32,1024]{3,2,1,0:T(8,128)} %fusion.127, f32[32,1,32,1023]{3,2,1,0:T(8,128)} %get-tuple-element.377, f32[32,1,32,1]{3,2,1,0:T(8,128)S(1)} %get-tuple-element.378, f32[32,1,32,1]{3,2,1,0:T(8,128)S(1)} %get-tuple-element.379, ...), kind=kLoop, calls=%fused_computation.16.clone.1 | loop fusion | flops 35651584 | bytes 42336512 | tf_op jit(solution)/shard_map/while/body/eval_jaxpr/sub | solution.py:51
  217.4 10.6 %convolution_bitcast_fusion.5 = f32[32,2,32,1024]{3,2,1,0:T(8,128)} fusion(f32[32,2,32,1024]{3,2,1,0:T(8,128)S(1)} %get-tuple-element.389, f32[32,32]{1,0:T(8,128)S(1)} %get-tuple-element.446), kind=kOutput, calls=%fused_computation.57.clone.1 | convolution fusion | flops 805306368 | bytes 16781312 | tf_op jit(solution)/shard_map/while/body/eval_jaxpr/rm,bcmn->bcrn/dot_general | solution.py:47
  228.1 13.4 %slice_subtract_fusion.5 = (f32[32,1,32,1024]{3,2,1,0:T(8,128)}, f32[32,1,32,1024]{3,2,1,0:T(8,128)}) fusion(f32[32,2,32,1024]{3,2,1,0:T(8,128)} %convolution_bitcast_fusion.5, f32[32,1,32,1023]{3,2,1,0:T(8,128)} %get-tuple-element.391, f32[32,1,32,1]{3,2,1,0:T(8,128)S(1)} %get-tuple-element.392, f32[32,1,32,1]{3,2,1,0:T(8,128)S(1)} %get-tuple-element.393, ...), kind=kLoop, calls=%fused_computation.10.clone.1 | loop fusion | flops 35651584 | bytes 42336512 | tf_op jit(solution)/shard_map/while/body/eval_jaxpr/sub | solution.py:51
  269.6 16.0 %fusion.128 = f32[4,128,32]{1,2,0:T(8,128)S(1)} fusion(f32[4,128,32]{1,2,0:T(8,128)S(1)} %get-tuple-element.422, s32[]{:T(128)} %get-tuple-element.421, bf16[128,65536]{1,0:T(8,128)(2,1)} %get-tuple-element.449, f32[32,65536]{1,0:T(8,128)} %bitcast.224, f32[32,65536]{1,0:T(8,128)} %reshape.513, f32[32,65536]{1,0:T(8,128)} %bitcast.225, ...), kind=kOutput, calls=%fused_computation.62.clone.1 | convolution fusion | flops 547356672 | bytes 41959432 | tf_op jit(solution)/shard_map/while/body/eval_jaxpr/dot_general | solution.py:114
  301.8 11.0 %fusion.127 = f32[32,2,32,1024]{3,2,1,0:T(8,128)} fusion(bf16[4,32,2,32,1024]{4,3,2,1,0:T(8,128)(2,1)} %get-tuple-element.440, s32[]{:T(128)} %get-tuple-element.421, f32[32,32]{1,0:T(8,128)S(1)} %get-tuple-element.446), kind=kOutput, calls=%fused_computation.58.clone.1 | convolution fusion | flops 805306368 | bytes 12587520 | tf_op jit(solution)/shard_map/while/body/eval_jaxpr/rm,bcmn->bcrn/dot_general | solution.py:47
  313.5 13.0 %slice_subtract_fusion.4 = (f32[32,1,32,1024]{3,2,1,0:T(8,128)}, f32[32,1,32,1024]{3,2,1,0:T(8,128)}) fusion(f32[32,2,32,1024]{3,2,1,0:T(8,128)} %fusion.127, f32[32,1,32,1023]{3,2,1,0:T(8,128)} %get-tuple-element.377, f32[32,1,32,1]{3,2,1,0:T(8,128)S(1)} %get-tuple-element.378, f32[32,1,32,1]{3,2,1,0:T(8,128)S(1)} %get-tuple-element.379, ...), kind=kLoop, calls=%fused_computation.16.clone.1 | loop fusion | flops 35651584 | bytes 42336512 | tf_op jit(solution)/shard_map/while/body/eval_jaxpr/sub | solution.py:51
  356.6 13.1 %slice_subtract_fusion.5 = (f32[32,1,32,1024]{3,2,1,0:T(8,128)}, f32[32,1,32,1024]{3,2,1,0:T(8,128)}) fusion(f32[32,2,32,1024]{3,2,1,0:T(8,128)} %convolution_bitcast_fusion.5, f32[32,1,32,1023]{3,2,1,0:T(8,128)} %get-tuple-element.391, f32[32,1,32,1]{3,2,1,0:T(8,128)S(1)} %get-tuple-element.392, f32[32,1,32,1]{3,2,1,0:T(8,128)S(1)} %get-tuple-element.393, ...), kind=kLoop, calls=%fused_computation.10.clone.1 | loop fusion | flops 35651584 | bytes 42336512 | tf_op jit(solution)/shard_map/while/body/eval_jaxpr/sub | solution.py:51
  397.9 16.0 %fusion.128 = f32[4,128,32]{1,2,0:T(8,128)S(1)} fusion(f32[4,128,32]{1,2,0:T(8,128)S(1)} %get-tuple-element.422, s32[]{:T(128)} %get-tuple-element.421, bf16[128,65536]{1,0:T(8,128)(2,1)} %get-tuple-element.449, f32[32,65536]{1,0:T(8,128)} %bitcast.224, f32[32,65536]{1,0:T(8,128)} %reshape.513, f32[32,65536]{1,0:T(8,128)} %bitcast.225, ...), kind=kOutput, calls=%fused_computation.62.clone.1 | convolution fusion | flops 547356672 | bytes 41959432 | tf_op jit(solution)/shard_map/while/body/eval_jaxpr/dot_general | solution.py:114
  430.3 11.0 %fusion.127 = f32[32,2,32,1024]{3,2,1,0:T(8,128)} fusion(bf16[4,32,2,32,1024]{4,3,2,1,0:T(8,128)(2,1)} %get-tuple-element.440, s32[]{:T(128)} %get-tuple-element.421, f32[32,32]{1,0:T(8,128)S(1)} %get-tuple-element.446), kind=kOutput, calls=%fused_computation.58.clone.1 | convolution fusion | flops 805306368 | bytes 12587520 | tf_op jit(solution)/shard_map/while/body/eval_jaxpr/rm,bcmn->bcrn/dot_general | solution.py:47
  442.0 13.0 %slice_subtract_fusion.4 = (f32[32,1,32,1024]{3,2,1,0:T(8,128)}, f32[32,1,32,1024]{3,2,1,0:T(8,128)}) fusion(f32[32,2,32,1024]{3,2,1,0:T(8,128)} %fusion.127, f32[32,1,32,1023]{3,2,1,0:T(8,128)} %get-tuple-element.377, f32[32,1,32,1]{3,2,1,0:T(8,128)S(1)} %get-tuple-element.378, f32[32,1,32,1]{3,2,1,0:T(8,128)S(1)} %get-tuple-element.379, ...), kind=kLoop, calls=%fused_computation.16.clone.1 | loop fusion | flops 35651584 | bytes 42336512 | tf_op jit(solution)/shard_map/while/body/eval_jaxpr/sub | solution.py:51
  474.3 10.6 %convolution_bitcast_fusion.5 = f32[32,2,32,1024]{3,2,1,0:T(8,128)} fusion(f32[32,2,32,1024]{3,2,1,0:T(8,128)S(1)} %get-tuple-element.389, f32[32,32]{1,0:T(8,128)S(1)} %get-tuple-element.446), kind=kOutput, calls=%fused_computation.57.clone.1 | convolution fusion | flops 805306368 | bytes 16781312 | tf_op jit(solution)/shard_map/while/body/eval_jaxpr/rm,bcmn->bcrn/dot_general | solution.py:47
  484.9 13.4 %slice_subtract_fusion.5 = (f32[32,1,32,1024]{3,2,1,0:T(8,128)}, f32[32,1,32,1024]{3,2,1,0:T(8,128)}) fusion(f32[32,2,32,1024]{3,2,1,0:T(8,128)} %convolution_bitcast_fusion.5, f32[32,1,32,1023]{3,2,1,0:T(8,128)} %get-tuple-element.391, f32[32,1,32,1]{3,2,1,0:T(8,128)S(1)} %get-tuple-element.392, f32[32,1,32,1]{3,2,1,0:T(8,128)S(1)} %get-tuple-element.393, ...), kind=kLoop, calls=%fused_computation.10.clone.1 | loop fusion | flops 35651584 | bytes 42336512 | tf_op jit(solution)/shard_map/while/body/eval_jaxpr/sub | solution.py:51
  526.5 16.0 %fusion.128 = f32[4,128,32]{1,2,0:T(8,128)S(1)} fusion(f32[4,128,32]{1,2,0:T(8,128)S(1)} %get-tuple-element.422, s32[]{:T(128)} %get-tuple-element.421, bf16[128,65536]{1,0:T(8,128)(2,1)} %get-tuple-element.449, f32[32,65536]{1,0:T(8,128)} %bitcast.224, f32[32,65536]{1,0:T(8,128)} %reshape.513, f32[32,65536]{1,0:T(8,128)} %bitcast.225, ...), kind=kOutput, calls=%fused_computation.62.clone.1 | convolution fusion | flops 547356672 | bytes 41959432 | tf_op jit(solution)/shard_map/while/body/eval_jaxpr/dot_general | solution.py:114
  550.6 11.7 %cholesky.19 = f32[128,128]{1,0:T(8,128)S(1)} custom-call(f32[128,128]{1,0:T(8,128)S(1)} %fusion.76), custom_call_target="Cholesky" | custom-call | tf_op jit(solution)/shard_map/jit(cholesky)/cholesky | solution.py:87
  590.0 11.0 %all-gather = f32[512,128]{1,0:T(8,128)S(1)} all-gather(f32[128,128]{1,0:T(8,128)S(1)} %fusion.45), channel_id=2, replica_groups=mesh['seq'=4,'grp'=32] {'seq'}, dimensions={0}, use_global_device_ids=true | all-gather | bytes 327680 | tf_op jit(solution)/shard_map/all_gather | solution.py:20
  601.7 52.5 %all-gather.4.cloned.1.call-done = f32[4096,128]{1,0:T(8,128)} async-done(((f32[128,128]{1,0:T(8,128)}), f32[4096,128]{1,0:T(8,128)}) %all-gather.4.cloned.1.call-update) | async-done | bytes 2097168 | tf_op jit(solution)/shard_map/all_gather | solution.py:134
  (185 shorter events, 326.8 us)
Async XLA Ops:
  7.2 647.0 %all-gather.4.cloned.1.call-start = ((), (), s32[]{:S(2)}) async-start(), calls=%async_computation | async-start | bytes 2162688 | tf_op jit(solution)/shard_map/all_gather | solution.py:134
  9.7 18.7 %copy-start.6 = (s32[32,2]{0,1:T(2,128)S(1)}, s32[32,2]{0,1:T(2,128)}, u32[]{:S(2)}) copy-start(s32[32,2]{0,1:T(2,128)} %param.12) | copy-start | bytes 772
  9.7 18.8 %copy-start = (f32[1,1,2,2,32,1024]{5,4,3,2,1,0:T(8,128)S(1)}, f32[1,1,2,2,32,1024]{5,4,3,2,1,0:T(8,128)}, u32[]{:S(2)}) copy-start(f32[1,1,2,2,32,1024]{5,4,3,2,1,0:T(8,128)} %param.9) | copy-start | bytes 1572868
  9.8 18.8 %copy-start.5 = (f32[32]{0:T(128)S(1)}, f32[32]{0:T(128)}, u32[]{:S(2)}) copy-start(f32[32]{0:T(128)} %param.10) | copy-start | bytes 388
  28.9 27.0 %copy-start.2 = (f32[1,32,1024]{2,1,0:T(8,128)}, f32[1,32,1024]{2,1,0:T(8,128)S(1)}, u32[]{:S(2)}) copy-start(f32[1,32,1024]{2,1,0:T(8,128)S(1)} %get-tuple-element.447) | copy-start | bytes 393220 | tf_op jit(solution)/shard_map/while
  44.9 11.0 %copy-start.4 = (f32[1,32,1024]{2,1,0:T(8,128)S(1)}, f32[1,32,1024]{2,1,0:T(8,128)}, u32[]{:S(2)}) copy-start(f32[1,32,1024]{2,1,0:T(8,128)} %get-tuple-element.443) | copy-start | bytes 393220 | tf_op jit(solution)/shard_map/while
  89.1 10.6 %copy-start.1 = (f32[1,32,1024]{2,1,0:T(8,128)S(1)}, f32[1,32,1024]{2,1,0:T(8,128)}, u32[]{:S(2)}) copy-start(f32[1,32,1024]{2,1,0:T(8,128)} %get-tuple-element.448) | copy-start | bytes 393220 | tf_op jit(solution)/shard_map/while
  117.4 8.1 %slice-start = ((s8[8388608]{0:T(1024)(128)(4,1)}), s8[4194304]{0:T(1024)(128)(4,1)S(1)}, s32[]{:S(2)}) async-start(s8[8388608]{0:T(1024)(128)(4,1)} %bitcast.220), calls=%async_computation.1 | async-start | bytes 8388608 | tf_op jit(solution)/shard_map/while
  141.0 16.0 %copy-start.3 = (f32[1,32,1024]{2,1,0:T(8,128)S(1)}, f32[1,32,1024]{2,1,0:T(8,128)}, u32[]{:S(2)}) copy-start(f32[1,32,1024]{2,1,0:T(8,128)} %copy-done.2) | copy-start | bytes 393220 | tf_op jit(solution)/shard_map/while
  157.5 27.0 %copy-start.2 = (f32[1,32,1024]{2,1,0:T(8,128)}, f32[1,32,1024]{2,1,0:T(8,128)S(1)}, u32[]{:S(2)}) copy-start(f32[1,32,1024]{2,1,0:T(8,128)S(1)} %get-tuple-element.447) | copy-start | bytes 393220 | tf_op jit(solution)/shard_map/while
  173.5 11.0 %copy-start.4 = (f32[1,32,1024]{2,1,0:T(8,128)S(1)}, f32[1,32,1024]{2,1,0:T(8,128)}, u32[]{:S(2)}) copy-start(f32[1,32,1024]{2,1,0:T(8,128)} %get-tuple-element.443) | copy-start | bytes 393220 | tf_op jit(solution)/shard_map/while
  217.4 10.6 %copy-start.1 = (f32[1,32,1024]{2,1,0:T(8,128)S(1)}, f32[1,32,1024]{2,1,0:T(8,128)}, u32[]{:S(2)}) copy-start(f32[1,32,1024]{2,1,0:T(8,128)} %get-tuple-element.448) | copy-start | bytes 393220 | tf_op jit(solution)/shard_map/while
  269.6 16.0 %copy-start.3 = (f32[1,32,1024]{2,1,0:T(8,128)S(1)}, f32[1,32,1024]{2,1,0:T(8,128)}, u32[]{:S(2)}) copy-start(f32[1,32,1024]{2,1,0:T(8,128)} %copy-done.2) | copy-start | bytes 393220 | tf_op jit(solution)/shard_map/while
  285.8 27.0 %copy-start.2 = (f32[1,32,1024]{2,1,0:T(8,128)}, f32[1,32,1024]{2,1,0:T(8,128)S(1)}, u32[]{:S(2)}) copy-start(f32[1,32,1024]{2,1,0:T(8,128)S(1)} %get-tuple-element.447) | copy-start | bytes 393220 | tf_op jit(solution)/shard_map/while
  301.8 11.0 %copy-start.4 = (f32[1,32,1024]{2,1,0:T(8,128)S(1)}, f32[1,32,1024]{2,1,0:T(8,128)}, u32[]{:S(2)}) copy-start(f32[1,32,1024]{2,1,0:T(8,128)} %get-tuple-element.443) | copy-start | bytes 393220 | tf_op jit(solution)/shard_map/while
  346.0 10.6 %copy-start.1 = (f32[1,32,1024]{2,1,0:T(8,128)S(1)}, f32[1,32,1024]{2,1,0:T(8,128)}, u32[]{:S(2)}) copy-start(f32[1,32,1024]{2,1,0:T(8,128)} %get-tuple-element.448) | copy-start | bytes 393220 | tf_op jit(solution)/shard_map/while
  397.9 16.0 %copy-start.3 = (f32[1,32,1024]{2,1,0:T(8,128)S(1)}, f32[1,32,1024]{2,1,0:T(8,128)}, u32[]{:S(2)}) copy-start(f32[1,32,1024]{2,1,0:T(8,128)} %copy-done.2) | copy-start | bytes 393220 | tf_op jit(solution)/shard_map/while
  414.4 27.0 %copy-start.2 = (f32[1,32,1024]{2,1,0:T(8,128)}, f32[1,32,1024]{2,1,0:T(8,128)S(1)}, u32[]{:S(2)}) copy-start(f32[1,32,1024]{2,1,0:T(8,128)S(1)} %get-tuple-element.447) | copy-start | bytes 393220 | tf_op jit(solution)/shard_map/while
  430.3 11.0 %copy-start.4 = (f32[1,32,1024]{2,1,0:T(8,128)S(1)}, f32[1,32,1024]{2,1,0:T(8,128)}, u32[]{:S(2)}) copy-start(f32[1,32,1024]{2,1,0:T(8,128)} %get-tuple-element.443) | copy-start | bytes 393220 | tf_op jit(solution)/shard_map/while
  474.3 10.6 %copy-start.1 = (f32[1,32,1024]{2,1,0:T(8,128)S(1)}, f32[1,32,1024]{2,1,0:T(8,128)}, u32[]{:S(2)}) copy-start(f32[1,32,1024]{2,1,0:T(8,128)} %get-tuple-element.448) | copy-start | bytes 393220 | tf_op jit(solution)/shard_map/while
  526.5 16.0 %copy-start.3 = (f32[1,32,1024]{2,1,0:T(8,128)S(1)}, f32[1,32,1024]{2,1,0:T(8,128)}, u32[]{:S(2)}) copy-start(f32[1,32,1024]{2,1,0:T(8,128)} %copy-done.2) | copy-start | bytes 393220 | tf_op jit(solution)/shard_map/while
  574.0 5.3 collective-permute-start
  579.6 5.0 collective-permute-start.1
  584.8 5.0 collective-permute-start.2
  (7 other events, 56.8 us)
Sparse Core Ops, SparseCore 0:
  601.8 52.3 all-gather.3
